TPU v7x, 32 devices: a whole 2x2x4 slice. The times are simulated.
32 devices in a mesh: dp: 8 (over y, x, core), seq: 4 (over z).
Axes of the slice: x: 2, y: 2, z: 4, core: 2. Of those that a mesh axis runs over, the one named last changes fastest.
Arguments:
- hidden_in: bfloat16 [8, 2048, 2048], P('dp', 'seq'), may hold values from -6 to 6
- memory: bfloat16 [8, 2048, 2048], P('dp', 'seq'), may hold values from -6 to 6
- segments: int32 [8, 2048], P('dp'), may hold values from 0 to 3, never falling along the last dimension, each value on 1 to 1200 neighbouring positions
- gain_attn: bfloat16 [2048], P(('dp', 'seq')), may hold values from 0.25 to 1.75
- w_query: bfloat16 [2048, 2048], P(('dp', 'seq')), may hold values from -0.125 to 0.125
- w_key: bfloat16 [2048, 2048], P(('dp', 'seq')), may hold values from -0.125 to 0.125
- w_value: bfloat16 [2048, 2048], P(('dp', 'seq')), may hold values from -0.125 to 0.125
- w_out: bfloat16 [2048, 2048], P(('dp', 'seq')), may hold values from -0.75 to 0.75
- gain_ffn: bfloat16 [2048], P(('dp', 'seq')), may hold values from 0.25 to 1.75
- w_gate: bfloat16 [5504, 2048], P(('dp', 'seq')), may hold values from -0.125 to 0.125
- w_up: bfloat16 [5504, 2048], P(('dp', 'seq')), may hold values from -0.125 to 0.125
- w_down: bfloat16 [5504, 2048], P(('dp', 'seq')), may hold values from -0.078125 to 0.078125
- cotangent: bfloat16 [8, 2048, 2048], P('dp', 'seq'), may hold values from -6 to 6
Outputs:
- layer_out: bfloat16 [8, 2048, 2048], P('dp', 'seq')
- grad_hidden: float32 [8, 2048, 2048], P('dp', 'seq')
- grad_memory: float32 [8, 2048, 2048], P('dp', 'seq')
- grad_gain_attn: float32 [2048], P(('dp', 'seq'))
- grad_w_query: float32 [2048, 2048], P(('dp', 'seq'))
- grad_w_key: float32 [2048, 2048], P(('dp', 'seq'))
- grad_w_value: float32 [2048, 2048], P(('dp', 'seq'))
- grad_w_out: float32 [2048, 2048], P(('dp', 'seq'))
- grad_gain_ffn: float32 [2048], P(('dp', 'seq'))
- grad_w_gate: float32 [5504, 2048], P(('dp', 'seq'))
- grad_w_up: float32 [5504, 2048], P(('dp', 'seq'))
- grad_w_down: float32 [5504, 2048], P(('dp', 'seq'))
Inputs may be any that keep to these rules, and one draw needn't show every extreme that they name: `segments`: along each sequence the numbers never fall; each number is held by 1 to 1200 consecutive tokens, and in every draw some document has exactly 1200.
All inputs are finite; a program needn't handle non-finite values.
Results may differ from a plain program's by a relative error of at most 0.019.
Values may be sent and summed in bfloat16 or wider, within the bound.
A program may use at most 384 MiB of HBM per device.

v0:
```python
import jax
import jax.numpy as jnp
from jax import lax
from jax.sharding import PartitionSpec as P

HEAD_DIM = 128
EPSILON = 1e-06
MASKED = -1e30


def rms_scale(values):
    return lax.rsqrt(jnp.mean(values * values, axis=-1, keepdims=True) + EPSILON)


def norm_back(grad_normed, normed, rstd, gain):
    scaled = grad_normed * gain
    return rstd * (scaled - normed * jnp.mean(scaled * normed, axis=-1, keepdims=True))


def visible(segment_ids, start, rows):
    length = segment_ids.shape[0]
    query_pos = start + lax.broadcasted_iota(jnp.int32, (rows, length), 0)
    key_pos = lax.broadcasted_iota(jnp.int32, (rows, length), 1)
    query_segment = lax.dynamic_slice_in_dim(segment_ids, start, rows)
    return (key_pos <= query_pos) & (query_segment[:, None] == segment_ids[None, :])


def block_scores(query_block, keys, segment_ids, start):
    rows = query_block.shape[0]
    scale = query_block.shape[2] ** (-0.5)
    score = (
        jnp.einsum("qhd,khd->hqk", query_block, keys, preferred_element_type=jnp.float32) * scale
    )
    return jnp.where(visible(segment_ids, start, rows)[None], score, MASKED)


def attend_forward(query, key, value, segment_ids):
    length, heads, width = query.shape
    rows = min(512, length)

    def one_block(index):
        start = index * rows
        query_block = lax.dynamic_slice_in_dim(query, start, rows, 0)
        score = block_scores(query_block, key, segment_ids, start)
        top = jnp.max(score, axis=-1, keepdims=True)
        raised = jnp.exp(score - top)
        total = jnp.sum(raised, axis=-1, keepdims=True)
        prob_low = (raised / total).astype(jnp.bfloat16)
        context = jnp.einsum("hqk,khd->qhd", prob_low, value, preferred_element_type=jnp.float32)
        return (context.astype(jnp.bfloat16), (top + jnp.log(total))[..., 0])

    context, logsum = lax.map(one_block, jnp.arange(length // rows, dtype=jnp.int32))
    return (context.reshape(length, heads * width), logsum)


def attend_backward(query, key, value, segment_ids, logsum, grad_context):
    length, heads, width = query.shape
    rows = min(512, length)
    scale = width ** (-0.5)

    def one_block(carry, index):
        grad_key, grad_value = carry
        start = index * rows
        query_block = lax.dynamic_slice_in_dim(query, start, rows, 0)
        grad_block = lax.dynamic_slice_in_dim(grad_context, start, rows, 0)
        score = block_scores(query_block, key, segment_ids, start)
        prob = jnp.exp(score - logsum[index][..., None])
        grad_value = grad_value + jnp.einsum(
            "hqk,qhd->khd",
            prob.astype(jnp.bfloat16),
            grad_block,
            preferred_element_type=jnp.float32,
        )
        grad_prob = jnp.einsum(
            "qhd,khd->hqk", grad_block, value, preferred_element_type=jnp.float32
        )
        grad_score = (
            prob * (grad_prob - jnp.sum(prob * grad_prob, axis=-1, keepdims=True))
        ).astype(jnp.bfloat16)
        grad_query = (
            jnp.einsum("hqk,khd->qhd", grad_score, key, preferred_element_type=jnp.float32) * scale
        )
        grad_key = (
            grad_key
            + jnp.einsum(
                "hqk,qhd->khd", grad_score, query_block, preferred_element_type=jnp.float32
            )
            * scale
        )
        return ((grad_key, grad_value), grad_query.astype(jnp.bfloat16))

    zeros = jnp.zeros((length, heads, width), jnp.float32)
    (grad_key, grad_value), grad_query = lax.scan(
        one_block, (zeros, zeros), jnp.arange(length // rows, dtype=jnp.int32)
    )
    flat = (length, heads * width)
    return (
        grad_query.reshape(flat),
        grad_key.astype(jnp.bfloat16).reshape(flat),
        grad_value.astype(jnp.bfloat16).reshape(flat),
    )


def row_terms(left, right, blocks, share):
    term = jnp.einsum("tk,td->kd", left, right, preferred_element_type=jnp.float32)
    return term.reshape(blocks, share, right.shape[1])


def gain_terms(vector, blocks):
    return jnp.broadcast_to(vector[None, None, :], (blocks, 1, vector.shape[0]))


def shards(
    hidden_in,
    memory,
    segments,
    gain_attn,
    w_query,
    w_key,
    w_value,
    w_out,
    gain_ffn,
    w_gate,
    w_up,
    w_down,
    cotangent,
):
    seqs, piece, width = hidden_in.shape
    groups = lax.axis_size("seq")
    dp_count = lax.axis_size("dp")
    length = piece * groups
    heads_here = width // groups // HEAD_DIM
    count = seqs * piece
    share_d = w_query.shape[0]
    share_f = w_gate.shape[0]
    tokens = hidden_in.reshape(count, width)
    memory_flat = memory.reshape(count, width)
    grad_out = cotangent.reshape(count, width)
    hidden32 = tokens.astype(jnp.float32)
    rstd_in = rms_scale(hidden32)
    normed_in = hidden32 * rstd_in
    gain_piece = lax.all_gather(gain_attn, ("dp", "seq"), axis=0, tiled=True)
    query_rows = lax.all_gather(w_query, ("dp", "seq"), axis=0, tiled=True)
    key_rows = lax.all_gather(w_key, ("dp", "seq"), axis=0, tiled=True)
    value_rows = lax.all_gather(w_value, ("dp", "seq"), axis=0, tiled=True)
    gain32 = gain_piece.astype(jnp.float32)
    columns = (normed_in * gain32).astype(jnp.bfloat16)
    query = jnp.dot(columns, query_rows, preferred_element_type=jnp.float32)
    key = jnp.dot(memory_flat, key_rows, preferred_element_type=jnp.float32)
    value = jnp.dot(memory_flat, value_rows, preferred_element_type=jnp.float32)
    attn_in = columns
    query, key, value, attn_in, gain_attn_full = (query, key, value, attn_in, gain32)
    cube = (seqs, piece, width)
    query_heads, key_heads, value_heads = (
        lax.all_to_all(
            query.astype(jnp.bfloat16).reshape(cube), "seq", split_axis=2, concat_axis=1, tiled=True
        ),
        lax.all_to_all(
            key.astype(jnp.bfloat16).reshape(cube), "seq", split_axis=2, concat_axis=1, tiled=True
        ),
        lax.all_to_all(
            value.astype(jnp.bfloat16).reshape(cube), "seq", split_axis=2, concat_axis=1, tiled=True
        ),
    )
    head_shape = (length, heads_here, HEAD_DIM)

    def forward_one(item):
        query_seq, key_seq, value_seq, segment_ids = item
        return attend_forward(
            query_seq.reshape(head_shape),
            key_seq.reshape(head_shape),
            value_seq.reshape(head_shape),
            segment_ids,
        )

    context_heads, logsum = lax.map(forward_one, (query_heads, key_heads, value_heads, segments))
    context = lax.all_to_all(context_heads, "seq", split_axis=1, concat_axis=2, tiled=True).reshape(
        count, width
    )
    out_full, gain_ffn_full = (
        lax.all_gather(w_out, ("dp", "seq"), axis=0, tiled=True),
        lax.all_gather(gain_ffn, ("dp", "seq"), axis=0, tiled=True),
    )
    mid = hidden32 + jnp.dot(context, out_full, preferred_element_type=jnp.float32)
    rstd_mid = rms_scale(mid)
    normed_mid = mid * rstd_mid
    gain_ffn32 = gain_ffn_full.astype(jnp.float32)
    ffn_in = (normed_mid * gain_ffn32).astype(jnp.bfloat16)
    gate_rows, up_rows = lax.all_gather((w_gate, w_up), ("dp", "seq"), axis=0, tiled=True)
    gate_part = jnp.einsum("td,fd->tf", ffn_in, gate_rows, preferred_element_type=jnp.float32)
    up_part = jnp.einsum("td,fd->tf", ffn_in, up_rows, preferred_element_type=jnp.float32)
    both = jnp.stack((gate_part, up_part))
    gate = both[0]
    up = both[1]
    gate_sigmoid = jax.nn.sigmoid(gate)
    act = (gate * gate_sigmoid * up).astype(jnp.bfloat16)
    columns = act
    branch = jnp.dot(
        columns,
        lax.all_gather(w_down, ("dp", "seq"), axis=0, tiled=True),
        preferred_element_type=jnp.float32,
    )
    layer_out = (mid + branch).astype(jnp.bfloat16).reshape(cube)
    grad_act = jnp.einsum(
        "td,fd->tf",
        grad_out,
        lax.all_gather(w_down, ("dp", "seq"), axis=0, tiled=True),
        preferred_element_type=jnp.float32,
    )
    grad_gate = (grad_act * up * gate_sigmoid * (1.0 + gate * (1.0 - gate_sigmoid))).astype(
        jnp.bfloat16
    )
    grad_up = (grad_act * gate * gate_sigmoid).astype(jnp.bfloat16)
    gate_rows = lax.all_gather(w_gate, ("dp", "seq"), axis=0, tiled=True)
    up_rows = lax.all_gather(w_up, ("dp", "seq"), axis=0, tiled=True)
    total = jnp.dot(grad_gate, gate_rows, preferred_element_type=jnp.float32)
    grad_ffn_in = total + jnp.dot(grad_up, up_rows, preferred_element_type=jnp.float32)
    grad_gain_ffn_all = jnp.sum(normed_mid * grad_ffn_in, axis=0)
    grad_mid = grad_out.astype(jnp.float32) + norm_back(
        grad_ffn_in, normed_mid, rstd_mid, gain_ffn32
    )
    grad_branch = grad_mid.astype(jnp.bfloat16)
    grad_context = jnp.einsum(
        "td,ed->te", grad_branch, out_full, preferred_element_type=jnp.float32
    ).astype(jnp.bfloat16)
    grad_context_heads = lax.all_to_all(
        grad_context.reshape(cube), "seq", split_axis=2, concat_axis=1, tiled=True
    )

    def backward_one(item):
        query_seq, key_seq, value_seq, segment_ids, logsum_seq, grad_seq = item
        return attend_backward(
            query_seq.reshape(head_shape),
            key_seq.reshape(head_shape),
            value_seq.reshape(head_shape),
            segment_ids,
            logsum_seq,
            grad_seq.reshape(head_shape),
        )

    grad_query_heads, grad_key_heads, grad_value_heads = lax.map(
        backward_one, (query_heads, key_heads, value_heads, segments, logsum, grad_context_heads)
    )
    grad_query, grad_key, grad_value = (
        lax.all_to_all(grad_query_heads, "seq", split_axis=1, concat_axis=2, tiled=True),
        lax.all_to_all(grad_key_heads, "seq", split_axis=1, concat_axis=2, tiled=True),
        lax.all_to_all(grad_value_heads, "seq", split_axis=1, concat_axis=2, tiled=True),
    )
    grad_query = grad_query.reshape(count, width)
    grad_key = grad_key.reshape(count, width)
    grad_value = grad_value.reshape(count, width)
    query_rows, key_rows, value_rows = lax.all_gather(
        (w_query, w_key, w_value), ("dp", "seq"), axis=0, tiled=True
    )
    grad_in = jnp.einsum("te,de->td", grad_query, query_rows, preferred_element_type=jnp.float32)
    grad_memory_part = jnp.einsum(
        "te,de->td", grad_key, key_rows, preferred_element_type=jnp.float32
    )
    grad_memory_part = grad_memory_part + jnp.einsum(
        "te,de->td", grad_value, value_rows, preferred_element_type=jnp.float32
    )
    both_grads = jnp.stack((grad_in, grad_memory_part))
    grad_attn_in = both_grads[0]
    grad_memory = both_grads[1].reshape(cube)
    grad_gain_attn_all = jnp.sum(normed_in * grad_attn_in, axis=0)
    grad_hidden = (grad_mid + norm_back(grad_attn_in, normed_in, rstd_in, gain_attn_full)).reshape(
        cube
    )
    gain_attn_group, gain_ffn_group = lax.psum((grad_gain_attn_all, grad_gain_ffn_all), "seq")

    def regroup(values):
        return values.reshape(count, dp_count, groups, values.shape[1] // (dp_count * groups))

    left_parts = (
        lax.all_to_all(regroup(attn_in), "seq", split_axis=2, concat_axis=0, tiled=True),
        lax.all_to_all(regroup(memory_flat), "seq", split_axis=2, concat_axis=0, tiled=True),
        lax.all_to_all(regroup(context), "seq", split_axis=2, concat_axis=0, tiled=True),
        lax.all_to_all(regroup(grad_gate), "seq", split_axis=2, concat_axis=0, tiled=True),
        lax.all_to_all(regroup(grad_up), "seq", split_axis=2, concat_axis=0, tiled=True),
        lax.all_to_all(regroup(act), "seq", split_axis=2, concat_axis=0, tiled=True),
    )
    whole_count = count * groups
    attn_left, memory_left, context_left, gate_left, up_left, act_left = [
        part.reshape(whole_count, part.shape[1] * part.shape[3]) for part in left_parts
    ]
    query_right, key_right, value_right, branch_right, ffn_right, out_right = (
        lax.all_gather(grad_query, "seq", axis=0, tiled=True),
        lax.all_gather(grad_key, "seq", axis=0, tiled=True),
        lax.all_gather(grad_value, "seq", axis=0, tiled=True),
        lax.all_gather(grad_branch, "seq", axis=0, tiled=True),
        lax.all_gather(ffn_in, "seq", axis=0, tiled=True),
        lax.all_gather(grad_out, "seq", axis=0, tiled=True),
    )
    attn_block = 4 * share_d + 1
    ffn_block = 3 * share_f + 1
    whole_block = attn_block + ffn_block
    blocks = whole_block * lax.axis_size("dp") // whole_block
    all_grads = lax.psum_scatter(
        jnp.concatenate(
            [
                row_terms(attn_left, query_right, blocks, share_d),
                row_terms(memory_left, key_right, blocks, share_d),
                row_terms(memory_left, value_right, blocks, share_d),
                row_terms(context_left, branch_right, blocks, share_d),
                gain_terms(gain_attn_group, blocks),
            ]
            + [
                row_terms(gate_left, ffn_right, blocks, share_f),
                row_terms(up_left, ffn_right, blocks, share_f),
                row_terms(act_left, out_right, blocks, share_f),
                gain_terms(gain_ffn_group, blocks),
            ],
            axis=1,
        )
        .reshape(whole_block * lax.axis_size("dp"), width)
        .astype(jnp.bfloat16),
        "dp",
        scatter_dimension=0,
        tiled=True,
    ).astype(jnp.float32)
    attn_grads = all_grads[:attn_block]
    ffn_grads = all_grads[attn_block:]
    owner = lax.axis_index("dp") * groups + lax.axis_index("seq")
    grad_w_query = attn_grads[0:share_d]
    grad_w_key = attn_grads[share_d : 2 * share_d]
    grad_w_value = attn_grads[2 * share_d : 3 * share_d]
    grad_w_out = attn_grads[3 * share_d : 4 * share_d]
    grad_gain_attn = lax.dynamic_slice_in_dim(attn_grads[4 * share_d], owner * share_d, share_d)
    grad_w_gate = ffn_grads[0:share_f]
    grad_w_up = ffn_grads[share_f : 2 * share_f]
    grad_w_down = ffn_grads[2 * share_f : 3 * share_f]
    grad_gain_ffn = lax.dynamic_slice_in_dim(ffn_grads[3 * share_f], owner * share_d, share_d)
    return (
        layer_out,
        grad_hidden,
        grad_memory,
        grad_gain_attn,
        grad_w_query,
        grad_w_key,
        grad_w_value,
        grad_w_out,
        grad_gain_ffn,
        grad_w_gate,
        grad_w_up,
        grad_w_down,
    )


def solution(mesh):
    in_specs = (
        P("dp", "seq", None),
        P("dp", "seq", None),
        P("dp", None),
        P(("dp", "seq")),
        P(("dp", "seq"), None),
        P(("dp", "seq"), None),
        P(("dp", "seq"), None),
        P(("dp", "seq"), None),
        P(("dp", "seq")),
        P(("dp", "seq"), None),
        P(("dp", "seq"), None),
        P(("dp", "seq"), None),
        P("dp", "seq", None),
    )
    out_specs = (
        P("dp", "seq", None),
        P("dp", "seq", None),
        P("dp", "seq", None),
        P(("dp", "seq")),
        P(("dp", "seq"), None),
        P(("dp", "seq"), None),
        P(("dp", "seq"), None),
        P(("dp", "seq"), None),
        P(("dp", "seq")),
        P(("dp", "seq"), None),
        P(("dp", "seq"), None),
        P(("dp", "seq"), None),
    )
    return jax.shard_map(shards, mesh=mesh, in_specs=in_specs, out_specs=out_specs, check_vma=False)
```

profile of v0, /device:TPU:1, one launch (start us, length us, event | category | flops | bytes accessed | tf_op | source)
XLA Modules:
  0.0 3069.0 jit_solution(8761035630606516971)
XLA Ops:
  13.6 42.0 %all-reduce.5 = (bf16[2048]{0:T(1024)(128)(2,1)S(1)}, bf16[2048]{0:T(1024)(128)(2,1)}) all-reduce(bf16[2048]{0:T(1024)(128)(2,1)S(1)} %dynamic-update-slice, bf16[2048]{0:T(1024)(128)(2,1)S(1)} %dynamic-update-slice.1), channel_id=1, replica_groups=mesh['dp'=8,'seq'=4] {'dp','seq'}, use_global_device_ids=true, to_apply=%add | all-reduce | flops 4096 | bytes 16384
  56.8 34.4 %all-gather.18.cloned.1.call-done = bf16[2048,2048]{1,0:T(8,128)(2,1)} async-done(((bf16[64,2048]{1,0:T(8,128)(2,1)}), bf16[2048,2048]{1,0:T(8,128)(2,1)}) %all-gather.18.cloned.1.call-update) | async-done | bytes 8388624 | tf_op jit(solution)/shard_map/all_gather | solution.py:143
  132.5 63.4 %all-gather.20.cloned.1.call-done = bf16[2048,2048]{1,0:T(8,128)(2,1)} async-done(((bf16[64,2048]{1,0:T(8,128)(2,1)}), bf16[2048,2048]{1,0:T(8,128)(2,1)}) %all-gather.20.cloned.1.call-update) | async-done | bytes 8388624 | tf_op jit(solution)/shard_map/all_gather | solution.py:144
  216.5 15.4 reduce.1
  244.7 63.4 %all-gather.22.cloned.1.call-done = bf16[2048,2048]{1,0:T(8,128)(2,1)} async-done(((bf16[64,2048]{1,0:T(8,128)(2,1)}), bf16[2048,2048]{1,0:T(8,128)(2,1)}) %all-gather.22.cloned.1.call-update) | async-done | bytes 8388624 | tf_op jit(solution)/shard_map/all_gather | solution.py:145
  328.7 15.4 reduce.2
  384.7 41.9 %all-to-all-done.2 = bf16[4,2,131072]{2,1,0:T(2,128)(2,1)} async-done(((bf16[4,2,131072]{2,1,0:T(2,128)(2,1)}), bf16[4,2,131072]{2,1,0:T(2,128)(2,1)}, u32[]{:S(2)}, u32[]{:S(2)}) %all-to-all-start.2) | async-done | bytes 2097184 | tf_op jit(solution)/shard_map/all_to_all | solution.py:161
  448.9 74.5 %while.47 = (s32[]{:T(128)}, bf16[4,512,4,128]{3,2,1,0:T(4,128)(2,1)}, f32[4,4,512]{2,1,0:T(4,128)}, s32[4]{0:T(128)S(1)}, s32[2048]{0:T(1024)S(1)}, /*index=5*/...) while((s32[]{:T(128)}, ...), condition=%wide.region_4.5_spmd, body=%wide.region_1.4_spmd.sunk | while | flops 2201221632 | bytes 69291224 | solution.py:52
  536.3 15.4 reduce.3
  560.0 67.4 %all-to-all-done.3 = bf16[4,2,131072]{2,1,0:T(2,128)(2,1)S(1)} async-done(((bf16[4,2,131072]{2,1,0:T(2,128)(2,1)}), bf16[4,2,131072]{2,1,0:T(2,128)(2,1)S(1)}, u32[]{:S(2)}, u32[]{:S(2)}) %all-to-all-start.3) | async-done | bytes 2097184 | tf_op jit(solution)/shard_map/all_to_all | solution.py:177
  663.2 23.0 reshape.356
  686.2 19.1 fusion.72
  705.3 70.9 %all-gather.40.cloned.1.call-done = bf16[32,172,2048]{2,1,0:T(8,128)(2,1)} async-done(((bf16[1,172,2048]{2,1,0:T(8,128)(2,1)}), bf16[32,172,2048]{2,1,0:T(8,128)(2,1)}) %all-gather.40.cloned.1.call-update) | async-done | bytes 22544400 | tf_op jit(solution)/shard_map/all_gather | solution.py:189
  776.2 22.2 reshape.358
  798.4 19.1 fusion.73
  817.5 104.3 %all-gather.42.cloned.1.call-done = bf16[32,172,2048]{2,1,0:T(8,128)(2,1)} async-done(((bf16[1,172,2048]{2,1,0:T(8,128)(2,1)}), bf16[32,172,2048]{2,1,0:T(8,128)(2,1)}) %all-gather.42.cloned.1.call-update) | async-done | bytes 22544400 | tf_op jit(solution)/shard_map/all_gather | solution.py:200
  921.8 22.4 reshape.360
  944.2 26.8 multiply_convert_fusion.1
  971.0 19.6 fusion.74
  990.7 21.8 multiply_reduce_fusion.1
  1061.5 87.5 %all-to-all-done.4 = bf16[4,2,131072]{2,1,0:T(2,128)(2,1)S(1)} async-done(((bf16[4,2,131072]{2,1,0:T(2,128)(2,1)}), bf16[4,2,131072]{2,1,0:T(2,128)(2,1)S(1)}, u32[]{:S(2)}, u32[]{:S(2)}) %all-to-all-start.4) | async-done | bytes 2097184 | tf_op jit(solution)/shard_map/all_to_all | solution.py:226
  1169.2 83.2 %all-to-all-done.9 = bf16[512,8,4,64]{0,3,1,2:T(8,128)(2,1)} async-done(((bf16[512,8,4,64]{0,3,1,2:T(8,128)(2,1)}), bf16[512,8,4,64]{0,3,1,2:T(8,128)(2,1)}, u32[]{:S(2)}, u32[]{:S(2)}) %all-to-all-start.9) | async-done | bytes 2097184 | tf_op jit(solution)/shard_map/all_to_all | solution.py:276
  1258.8 274.2 %while.48 = (s32[]{:T(128)}, f32[2048,4,128]{0,2,1:T(8,128)}, f32[2048,4,128]{0,2,1:T(8,128)}, bf16[4,512,4,128]{3,2,1,0:T(4,128)(2,1)}, s32[4]{0:T(128)S(1)}, /...) while((s32[]{:T(128)}, f32[2048,4,128]{0,2,1:T(8,128)}, ...), condition=%wide.region_9.10_spmd.clone, body=%wide.region_7.9_spmd.clone.sunk | while | flops 5440535040 | bytes 193538896 | solution.py:93
  1288.3 15.0 multiply_convert_fusion.9
  1355.4 15.0 multiply_convert_fusion.9
  1424.4 15.2 multiply_convert_fusion.9
  1493.5 14.9 multiply_convert_fusion.9
  1576.9 15.4 reduce.5
  1596.9 15.2 all-to-all-done.6
  1652.0 45.8 %all-to-all-done.5 = bf16[4,2,131072]{2,1,0:T(2,128)(2,1)} async-done(((bf16[4,2,131072]{2,1,0:T(2,128)(2,1)}), bf16[4,2,131072]{2,1,0:T(2,128)(2,1)}, u32[]{:S(2)}, u32[]{:S(2)}) %all-to-all-start.5) | async-done | bytes 2097184 | tf_op jit(solution)/shard_map/all_to_all | solution.py:245
  1701.8 29.0 reshape.365
  1730.8 14.5 copy.166
  1745.4 54.4 %all-to-all-done.7 = bf16[4,2,131072]{2,1,0:T(2,128)(2,1)S(1)} async-done(((bf16[4,2,131072]{2,1,0:T(2,128)(2,1)}), bf16[4,2,131072]{2,1,0:T(2,128)(2,1)S(1)}, u32[]{:S(2)}, u32[]{:S(2)}) %all-to-all-start.7) | async-done | bytes 2097184 | tf_op jit(solution)/shard_map/all_to_all | solution.py:247
  1813.4 29.1 reshape.366
  1842.5 14.5 copy.169
  1857.1 163.9 %all-to-all-done.11 = bf16[512,8,4,172]{0,1,3,2:T(8,128)(2,1)} async-done(((bf16[512,8,4,172]{0,1,3,2:T(8,128)(2,1)}), bf16[512,8,4,172]{0,1,3,2:T(8,128)(2,1)}, u32[]{:S(2)}, u32[]{:S(2)}) %all-to-all-start.11) | async-done | bytes 5636128 | tf_op jit(solution)/shard_map/all_to_all | solution.py:278
  2026.3 29.1 reshape.367
  2055.4 14.5 copy.172
  2069.9 151.5 %all-to-all-done.12 = bf16[512,8,4,172]{0,1,3,2:T(8,128)(2,1)} async-done(((bf16[512,8,4,172]{0,1,3,2:T(8,128)(2,1)}), bf16[512,8,4,172]{0,1,3,2:T(8,128)(2,1)}, u32[]{:S(2)}, u32[]{:S(2)}) %all-to-all-start.12) | async-done | bytes 5636128 | tf_op jit(solution)/shard_map/all_to_all | solution.py:279
  2243.7 18.0 fusion.57
  2284.0 154.2 %all-reduce.4 = (bf16[2048]{0:T(1024)(128)(2,1)S(1)}, bf16[2048]{0:T(1024)(128)(2,1)S(1)}) all-reduce(f32[2048]{0:T(1024)S(1)} %get-tuple-element.284, f32[2048]{0:T(1024)S(1)} %copy-done.35), channel_id=1, replica_groups=mesh['dp'=8,'seq'=4] {'seq'}, use_global_device_ids=true, to_apply=%region_12.13 | all-reduce | flops 4096 | bytes 24576 | tf_op jit(solution)/shard_map/psum | solution.py:269
  2510.0 18.4 fusion.41
  2528.4 15.9 fusion.44
  2544.2 18.0 fusion.47
  2600.8 143.7 %concatenate.4 = bf16[8,774,2048]{2,1,0:T(8,128)(2,1)} concatenate(bf16[8,64,2048]{2,1,0:T(8,128)(2,1)} %fusion.51, bf16[8,64,2048]{2,1,0:T(8,128)(2,1)} %bitcast.343, bf16[8,64,2048]{2,1,0:T(8,128)(2,1)} %bitcast.344, bf16[8,64,2048]{2,1,0:T(8,128)(2,1)S(1)} %fusion.54, bf16[8,1,2048]{2,1,0:T(2,128)(2,1)S(1)} %broadcast_in_dim.83, bf16[8,172,2048]{2,1,0:T(8,128)(2,1)} %fusion.41, ...), dimensions={1} | concatenate | bytes 50724864 | tf_op jit(solution)/shard_map/concatenate | solution.py:299
  2744.5 25.0 convert_element_type.114
  2769.5 258.1 %fusion = bf16[784,2048]{1,0:T(8,128)(2,1)} fusion(bf16[6192,2048]{1,0:T(8,128)(2,1)} %convert_element_type.114), kind=kCustom, calls=%all-reduce-scatter | all-reduce-scatter fusion | flops 12845057 | bytes 28574208
  3040.9 16.2 concatenate.5
  (359 shorter events, 855.9 us)
Async XLA Ops:
  7.2 49.1 %copy-start.8 = (bf16[1,512,2048]{2,1,0:T(8,128)(2,1)S(1)}, bf16[1,512,2048]{2,1,0:T(8,128)(2,1)}, u32[]{:S(2)}) copy-start(bf16[1,512,2048]{2,1,0:T(8,128)(2,1)} %param.17) | copy-start | bytes 6291460
  7.2 83.9 %all-gather.18.cloned.1.call-start = ((), (), s32[]{:S(2)}) async-start(), calls=%async_computation.14 | async-start | bytes 8650752 | tf_op jit(solution)/shard_map/all_gather | solution.py:143
  7.9 188.0 %all-gather.20.cloned.1.call-start = ((), (), s32[]{:S(2)}) async-start(), calls=%async_computation.15 | async-start | bytes 8650752 | tf_op jit(solution)/shard_map/all_gather | solution.py:144
  8.7 299.5 %all-gather.22.cloned.1.call-start = ((), (), s32[]{:S(2)}) async-start(), calls=%async_computation.16 | async-start | bytes 8650752 | tf_op jit(solution)/shard_map/all_gather | solution.py:145
  9.4 629.7 %all-gather.24.cloned.1.call-start = ((), (), s32[]{:S(2)}) async-start(), calls=%async_computation.17 | async-start | bytes 8650752 | tf_op jit(solution)/shard_map/all_gather | solution.py:181
  10.0 653.2 %all-gather.38.cloned.1.call-start = ((), (), s32[]{:S(2)}) async-start(), calls=%async_computation.24 | async-start | bytes 23789568 | tf_op jit(solution)/shard_map/all_gather | solution.py:189
  10.6 765.6 %all-gather.40.cloned.1.call-start = ((), (), s32[]{:S(2)}) async-start(), calls=%async_computation.25 | async-start | bytes 23789568 | tf_op jit(solution)/shard_map/all_gather | solution.py:189
  11.1 910.7 %all-gather.42.cloned.1.call-start = ((), (), s32[]{:S(2)}) async-start(), calls=%async_computation.26 | async-start | bytes 23789568 | tf_op jit(solution)/shard_map/all_gather | solution.py:200
  56.3 44.1 %copy-start.23 = (f32[2048]{0:T(1024)}, f32[2048]{0:T(1024)S(1)}, u32[]{:S(2)}) copy-start(f32[2048]{0:T(1024)S(1)} %convert_element_type.95) | copy-start | bytes 24580
  56.8 43.6 %copy-start.26 = (f32[512]{0:T(512)}, f32[512]{0:T(512)S(1)}, u32[]{:S(2)}) copy-start(f32[512]{0:T(512)S(1)} %add_rsqrt_fusion.1) | copy-start | bytes 6148
  128.4 107.9 %all-to-all-start = ((bf16[4,2,131072]{2,1,0:T(2,128)(2,1)}), bf16[4,2,131072]{2,1,0:T(2,128)(2,1)S(1)}, u32[]{:S(2)}, u32[]{:S(2)}) async-start(bf16[4,2,131072]{2,1,0:T(2,128)(2,1)} %reshape.369), calls=%async_computation | async-start | bytes 4194304 | tf_op jit(solution)/shard_map/all_to_all | solution.py:155
  236.3 112.3 %all-to-all-start.1 = ((bf16[4,2,131072]{2,1,0:T(2,128)(2,1)}), bf16[4,2,131072]{2,1,0:T(2,128)(2,1)}, u32[]{:S(2)}, u32[]{:S(2)}) async-start(bf16[4,2,131072]{2,1,0:T(2,128)(2,1)} %reshape.371), calls=%async_computation.1 | async-start | bytes 4194304 | tf_op jit(solution)/shard_map/all_to_all | solution.py:158
  348.6 78.0 %all-to-all-start.2 = ((bf16[4,2,131072]{2,1,0:T(2,128)(2,1)}), bf16[4,2,131072]{2,1,0:T(2,128)(2,1)}, u32[]{:S(2)}, u32[]{:S(2)}) async-start(bf16[4,2,131072]{2,1,0:T(2,128)(2,1)} %reshape.373), calls=%async_computation.2 | async-start | bytes 4194304 | tf_op jit(solution)/shard_map/all_to_all | solution.py:161
  523.4 28.3 copy-start.1
  556.3 71.1 %all-to-all-start.3 = ((bf16[4,2,131072]{2,1,0:T(2,128)(2,1)}), bf16[4,2,131072]{2,1,0:T(2,128)(2,1)S(1)}, u32[]{:S(2)}, u32[]{:S(2)}) async-start(bf16[4,2,131072]{2,1,0:T(2,128)(2,1)} %reshape.375), calls=%async_computation.3 | async-start | bytes 4194304 | tf_op jit(solution)/shard_map/all_to_all | solution.py:177
  559.9 1950.0 %all-gather.34.cloned.1.call-start = ((), (), s32[]{:S(2)}) async-start(), calls=%async_computation.22 | async-start | bytes 10485760 | tf_op jit(solution)/shard_map/all_gather | solution.py:291
  560.0 86.9 %copy-start.17 = (f32[2048]{0:T(1024)}, f32[2048]{0:T(1024)S(1)}, u32[]{:S(2)}) copy-start(f32[2048]{0:T(1024)S(1)} %convert_element_type.100) | copy-start | bytes 24580
  658.0 392.9 %all-to-all-start.8 = ((bf16[512,8,4,64]{0,3,1,2:T(8,128)(2,1)}), bf16[512,8,4,64]{0,3,1,2:T(8,128)(2,1)}, u32[]{:S(2)}, u32[]{:S(2)}) async-start(bf16[512,8,4,64]{0,3,1,2:T(8,128)(2,1)} %copy.157), calls=%async_computation.8 | async-start | bytes 4194304 | tf_op jit(solution)/shard_map/all_to_all | solution.py:275
  662.4 1881.8 %all-gather.36.cloned.1.call-start = ((), (), s32[]{:S(2)}) async-start(), calls=%async_computation.23 | async-start | bytes 10485760 | tf_op jit(solution)/shard_map/all_gather | solution.py:292
  663.1 23.0 copy-start.13
  817.5 126.7 %copy-start.12 = (bf16[1,512,2048]{2,1,0:T(8,128)(2,1)S(1)}, bf16[1,512,2048]{2,1,0:T(8,128)(2,1)}, u32[]{:S(2)}) copy-start(bf16[1,512,2048]{2,1,0:T(8,128)(2,1)} %param.29) | copy-start | bytes 6291460
  971.0 19.7 copy-start.6
  971.0 19.7 copy-start.18
  971.0 19.7 copy-start.21
  1050.8 98.1 %all-to-all-start.4 = ((bf16[4,2,131072]{2,1,0:T(2,128)(2,1)}), bf16[4,2,131072]{2,1,0:T(2,128)(2,1)S(1)}, u32[]{:S(2)}, u32[]{:S(2)}) async-start(bf16[4,2,131072]{2,1,0:T(2,128)(2,1)} %reshape.377), calls=%async_computation.4 | async-start | bytes 4194304 | tf_op jit(solution)/shard_map/all_to_all | solution.py:226
  1149.0 103.5 %all-to-all-start.9 = ((bf16[512,8,4,64]{0,3,1,2:T(8,128)(2,1)}), bf16[512,8,4,64]{0,3,1,2:T(8,128)(2,1)}, u32[]{:S(2)}, u32[]{:S(2)}) async-start(bf16[512,8,4,64]{0,3,1,2:T(8,128)(2,1)} %copy.160), calls=%async_computation.9 | async-start | bytes 4194304 | tf_op jit(solution)/shard_map/all_to_all | solution.py:276
  1153.5 1408.8 %all-gather.32.cloned.1.call-start = ((), (), s32[]{:S(2)}) async-start(), calls=%async_computation.21 | async-start | bytes 10485760 | tf_op jit(solution)/shard_map/all_gather | solution.py:290
  1169.2 89.6 %copy-start.2 = (bf16[2048,4,128]{2,0,1:T(8,128)(2,1)S(1)}, bf16[2048,4,128]{2,0,1:T(8,128)(2,1)}, u32[]{:S(2)}) copy-start(bf16[2048,4,128]{2,0,1:T(8,128)(2,1)} %copy-done.1) | copy-start | bytes 6291460
  1169.2 89.6 %copy-start.16 = (s32[1,2048]{1,0:T(1,128)S(1)}, s32[1,2048]{1,0:T(1,128)}, u32[]{:S(2)}) copy-start(s32[1,2048]{1,0:T(1,128)} %param.19) | copy-start | bytes 24580
  1252.4 307.5 %all-to-all-start.10 = ((bf16[512,8,4,64]{0,3,1,2:T(8,128)(2,1)}), bf16[512,8,4,64]{0,3,1,2:T(8,128)(2,1)}, u32[]{:S(2)}, u32[]{:S(2)}) async-start(bf16[512,8,4,64]{0,3,1,2:T(8,128)(2,1)} %copy.163), calls=%async_computation.10 | async-start | bytes 4194304 | tf_op jit(solution)/shard_map/all_to_all | solution.py:277
  1559.9 52.1 %all-to-all-start.6 = ((bf16[4,2,131072]{2,1,0:T(2,128)(2,1)}), bf16[4,2,131072]{2,1,0:T(2,128)(2,1)S(1)}, u32[]{:S(2)}, u32[]{:S(2)}) async-start(bf16[4,2,131072]{2,1,0:T(2,128)(2,1)} %reshape.381), calls=%async_computation.6 | async-start | bytes 4194304 | tf_op jit(solution)/shard_map/all_to_all | solution.py:246
  1612.0 85.7 %all-to-all-start.5 = ((bf16[4,2,131072]{2,1,0:T(2,128)(2,1)}), bf16[4,2,131072]{2,1,0:T(2,128)(2,1)}, u32[]{:S(2)}, u32[]{:S(2)}) async-start(bf16[4,2,131072]{2,1,0:T(2,128)(2,1)} %reshape.379), calls=%async_computation.5 | async-start | bytes 4194304 | tf_op jit(solution)/shard_map/all_to_all | solution.py:245
  1616.5 954.4 %all-gather.28.cloned.1.call-start = ((), (), s32[]{:S(2)}) async-start(), calls=%async_computation.19 | async-start | bytes 10485760 | tf_op jit(solution)/shard_map/all_gather | solution.py:288
  1697.8 102.0 %all-to-all-start.7 = ((bf16[4,2,131072]{2,1,0:T(2,128)(2,1)}), bf16[4,2,131072]{2,1,0:T(2,128)(2,1)S(1)}, u32[]{:S(2)}, u32[]{:S(2)}) async-start(bf16[4,2,131072]{2,1,0:T(2,128)(2,1)} %reshape.383), calls=%async_computation.7 | async-start | bytes 4194304 | tf_op jit(solution)/shard_map/all_to_all | solution.py:247
  1799.8 221.2 %all-to-all-start.11 = ((bf16[512,8,4,172]{0,1,3,2:T(8,128)(2,1)}), bf16[512,8,4,172]{0,1,3,2:T(8,128)(2,1)}, u32[]{:S(2)}, u32[]{:S(2)}) async-start(bf16[512,8,4,172]{0,1,3,2:T(8,128)(2,1)} %copy.166), calls=%async_computation.11 | async-start | bytes 11272192 | tf_op jit(solution)/shard_map/all_to_all | solution.py:278
  1804.9 775.9 %all-gather.30.cloned.1.call-start = ((), (), s32[]{:S(2)}) async-start(), calls=%async_computation.20 | async-start | bytes 10485760 | tf_op jit(solution)/shard_map/all_gather | solution.py:289
  2020.9 200.5 %all-to-all-start.12 = ((bf16[512,8,4,172]{0,1,3,2:T(8,128)(2,1)}), bf16[512,8,4,172]{0,1,3,2:T(8,128)(2,1)}, u32[]{:S(2)}, u32[]{:S(2)}) async-start(bf16[512,8,4,172]{0,1,3,2:T(8,128)(2,1)} %copy.169), calls=%async_computation.12 | async-start | bytes 11272192 | tf_op jit(solution)/shard_map/all_to_all | solution.py:279
  2069.9 156.7 %copy-start.37 = (u32[32]{0:T(128)S(1)}, u32[32]{0:T(128)}, u32[]{:S(2)}) copy-start(u32[32]{0:T(128)} %constant.133) | copy-start | bytes 388
  2221.4 270.8 %all-to-all-start.13 = ((bf16[512,8,4,172]{0,1,3,2:T(8,128)(2,1)}), bf16[512,8,4,172]{0,1,3,2:T(8,128)(2,1)}, u32[]{:S(2)}, u32[]{:S(2)}) async-start(bf16[512,8,4,172]{0,1,3,2:T(8,128)(2,1)} %copy.172), calls=%async_computation.13 | async-start | bytes 11272192 | tf_op jit(solution)/shard_map/all_to_all | solution.py:280
  2226.5 364.0 %all-gather.26.cloned.1.call-start = ((), (), s32[]{:S(2)}) async-start(), calls=%async_computation.18 | async-start | bytes 10485760 | tf_op jit(solution)/shard_map/all_gather | solution.py:287
  2769.5 263.6 %copy-start.11 = (bf16[1,512,2048]{2,1,0:T(8,128)(2,1)S(1)}, bf16[1,512,2048]{2,1,0:T(8,128)(2,1)}, u32[]{:S(2)}) copy-start(bf16[1,512,2048]{2,1,0:T(8,128)(2,1)} %param.17) | copy-start | bytes 6291460
  2769.5 263.6 %copy-start.19 = (f32[2048]{0:T(1024)S(1)}, f32[2048]{0:T(1024)}, u32[]{:S(2)}) copy-start(f32[2048]{0:T(1024)} %copy-done.17) | copy-start | bytes 24580
  2769.5 263.6 %copy-start.22 = (f32[512]{0:T(512)S(1)}, f32[512]{0:T(512)}, u32[]{:S(2)}) copy-start(f32[512]{0:T(512)} %copy-done.20) | copy-start | bytes 6148
  2769.5 263.6 %copy-start.25 = (f32[2048]{0:T(1024)S(1)}, f32[2048]{0:T(1024)}, u32[]{:S(2)}) copy-start(f32[2048]{0:T(1024)} %copy-done.23) | copy-start | bytes 24580
  2769.5 263.6 %copy-start.29 = (f32[512]{0:T(512)S(1)}, f32[512]{0:T(512)}, u32[]{:S(2)}) copy-start(f32[512]{0:T(512)} %copy-done.26) | copy-start | bytes 6148
  2769.5 263.6 %copy-start.31 = (f32[512]{0:T(512)S(1)}, f32[512]{0:T(512)}, u32[]{:S(2)}) copy-start(f32[512]{0:T(512)} %copy-done.30) | copy-start | bytes 6148
  2769.5 263.6 %copy-start.34 = (f32[512]{0:T(512)S(1)}, f32[512]{0:T(512)}, u32[]{:S(2)}) copy-start(f32[512]{0:T(512)} %broadcast_multiply_fusion) | copy-start | bytes 6148
  3028.7 12.3 collective-permute-start
  (30 other events, 168.0 us)
Sparse Core Ops, SparseCore 0:
  11.0 80.1 all-gather.17
  94.0 101.7 all-gather.19
  198.8 109.2 all-gather.21
  310.9 108.5 all-gather.23
  422.2 161.5 all-gather.37
  586.4 189.6 all-gather.39
  779.0 142.7 all-gather.41
  923.4 165.5 all-gather.33
  1090.5 250.3 all-gather.35
  1342.3 147.7 all-gather.31
  1625.1 307.7 all-gather.27
  1934.3 272.3 all-gather.29
  2273.2 213.7 all-gather.25
where the time goes:
time: 3090 us; the launch traced here: 3070 us
  waiting for transfers between devices  1050 us (34%)
  local copies, waits for them, and re-layouts  719 us (23%)
  matrix products  509 us (16%)
  blocking collectives  454 us (15%)
  other arithmetic  230 us (7%)
  starting transfers between devices  73.9 us (2%)
    unnamed x2, blocking collectives  300 us
    unnamed x119, local copies, waits for them, and re-layouts  203 us
    all_to_all x1, waiting for transfers between devices, shards(): lax.all_to_all(regroup(grad_gate), 'seq', split_axis=2, concat_axis=0, ti...  164 us
    psum x1, blocking collectives, shards(): lax.psum((grad_gain_attn_all, grad_gain_ffn_all), 'seq')  154 us
    all_to_all x1, waiting for transfers between devices, shards(): lax.all_to_all(regroup(grad_up), 'seq', split_axis=2, concat_axis=0, tile...  152 us
    concatenate x1, local copies, waits for them, and re-layouts, shards(): jnp.concatenate([row_terms(attn_left, query_right, blocks, share_d), row_...  144 us
    reshape x6, local copies, waits for them, and re-layouts, regroup(): values.reshape(count, dp_count, groups, values.shape[1] // (dp_count * gr...  131 us
    unnamed x11, other arithmetic  118 us
  transfers between devices with their start and end apart: 28, of which 14 were waited for; matrix products, arithmetic and copies ran while one was open for 41% of the time, Pallas kernels for 0%

commit v1 on v0

--- a/solution.py
+++ b/solution.py
@@ -6,6 +6,28 @@
 HEAD_DIM = 128
 EPSILON = 1e-06
 MASKED = -1e30
+
+
+def cut_along(x, dim, size):
+    before, after = (x.shape[:dim], x.shape[dim + 1 :])
+    return jnp.moveaxis(x.reshape(*before, size, -1, *after), dim, 0)
+
+
+def joined_along(blocks, dim):
+    dims = list(blocks.shape[1:])
+    dims[dim] *= blocks.shape[0]
+    return jnp.moveaxis(blocks, 0, dim).reshape(dims)
+
+
+def pairwise_exchange(shard, axis, split_dim, concat_dim):
+    size, index = (lax.axis_size(axis), lax.axis_index(axis))
+    blocks = cut_along(shard, split_dim, size)
+    outs = [blocks[index]]
+    for step in range(1, size):
+        sent = blocks[index ^ step]
+        outs.append(lax.ppermute(sent, axis, [(i, i ^ step) for i in range(size)]))
+    blocks = jnp.stack(outs)[index ^ jnp.arange(size)]
+    return joined_along(blocks, concat_dim)
 
 
 def rms_scale(values):
@@ -275,7 +297,7 @@
         lax.all_to_all(regroup(attn_in), "seq", split_axis=2, concat_axis=0, tiled=True),
         lax.all_to_all(regroup(memory_flat), "seq", split_axis=2, concat_axis=0, tiled=True),
         lax.all_to_all(regroup(context), "seq", split_axis=2, concat_axis=0, tiled=True),
-        lax.all_to_all(regroup(grad_gate), "seq", split_axis=2, concat_axis=0, tiled=True),
+        pairwise_exchange(regroup(grad_gate), "seq", 2, 0),
         lax.all_to_all(regroup(grad_up), "seq", split_axis=2, concat_axis=0, tiled=True),
         lax.all_to_all(regroup(act), "seq", split_axis=2, concat_axis=0, tiled=True),
     )

time: 3090 us -> 2960 us (0.958)
  blocking collectives: 454 us -> 369 us
  waiting for transfers between devices: 1050 us -> 1010 us
    all_to_all x1 -> x0, waiting for transfers between devices: 164 us -> none  [shards(): lax.all_to_all(regroup(grad_gate), 'seq', split_axis=2, concat_axis=0, ti...]
    ppermute x0 -> x3, waiting for transfers between devices: none -> 91.9 us  [pairwise_exchange(): outs.append(lax.ppermute(sent, axis, [(i, i ^ step) for i in range(size)]))]
    psum x1, blocking collectives: 154 us -> 73.7 us  [shards(): lax.psum((grad_gain_attn_all, grad_gain_ffn_all), 'seq')]
    all_to_all x1, waiting for transfers between devices: 0.01 us -> 74.9 us  [shards(): lax.all_to_all(regroup(context), 'seq', split_axis=2, concat_axis=0, tile...]
    all_to_all x1, waiting for transfers between devices: 54.4 us -> 3.39 us  [shards(): lax.all_to_all(grad_value_heads, 'seq', split_axis=1, concat_axis=2, tile...]
    reshape x6 -> x4, local copies, waits for them, and re-layouts: 131 us -> 87.1 us  [regroup(): values.reshape(count, dp_count, groups, values.shape[1] // (dp_count * gr...]
    unnamed x119 -> x107, local copies, waits for them, and re-layouts: 203 us -> 205 us
    unnamed x11 -> x10, other arithmetic: 118 us -> 118 us
  transfers between devices with their start and end apart: 28 -> 30, of which waited for: 14 -> 16; matrix products, arithmetic and copies ran while one was open for 41% -> 43% of each run, Pallas kernels for 0% -> 0%
where the time goes in v1:
time: 2960 us; the launch traced here: 2940 us
  waiting for transfers between devices  1010 us (34%)
  local copies, waits for them, and re-layouts  707 us (24%)
  matrix products  518 us (18%)
  blocking collectives  369 us (12%)
  other arithmetic  236 us (8%)
  starting transfers between devices  72.8 us (2%)
    unnamed x2, blocking collectives  296 us
    unnamed x107, local copies, waits for them, and re-layouts  205 us
    all_to_all x1, waiting for transfers between devices, shards(): lax.all_to_all(regroup(grad_up), 'seq', split_axis=2, concat_axis=0, tile...  168 us
    concatenate x1, local copies, waits for them, and re-layouts, shards(): jnp.concatenate([row_terms(attn_left, query_right, blocks, share_d), row_...  148 us
    unnamed x10, other arithmetic  118 us
    all_gather x1, waiting for transfers between devices, shards(): lax.all_gather(w_down, ('dp', 'seq'), axis=0, tiled=True)  104 us
    dot_general x7, matrix products, row_terms(): jnp.einsum('tk,td->kd', left, right, preferred_element_type=jnp.float32)  93.9 us
    ppermute x3, waiting for transfers between devices, pairwise_exchange(): outs.append(lax.ppermute(sent, axis, [(i, i ^ step) for i in range(size)]))  91.9 us
  transfers between devices with their start and end apart: 30, of which 16 were waited for; matrix products, arithmetic and copies ran while one was open for 43% of the time, Pallas kernels for 0%

profile of v1, /device:TPU:1, one launch (start us, length us, event | category | flops | bytes accessed | tf_op | source)
XLA Modules:
  0.0 2943.0 jit_solution(6151377399203111694)
XLA Ops:
  13.6 42.0 %all-reduce.5 = (bf16[2048]{0:T(1024)(128)(2,1)S(1)}, bf16[2048]{0:T(1024)(128)(2,1)}) all-reduce(bf16[2048]{0:T(1024)(128)(2,1)S(1)} %dynamic-update-slice, bf16[2048]{0:T(1024)(128)(2,1)S(1)} %dynamic-update-slice.1), channel_id=1, replica_groups=mesh['dp'=8,'seq'=4] {'dp','seq'}, use_global_device_ids=true, to_apply=%add | all-reduce | flops 4096 | bytes 16384
  56.8 34.4 %all-gather.18.cloned.1.call-done = bf16[2048,2048]{1,0:T(8,128)(2,1)} async-done(((bf16[64,2048]{1,0:T(8,128)(2,1)}), bf16[2048,2048]{1,0:T(8,128)(2,1)}) %all-gather.18.cloned.1.call-update) | async-done | bytes 8388624 | tf_op jit(solution)/shard_map/all_gather | solution.py:165
  111.6 14.1 reduce
  132.2 63.3 %all-gather.20.cloned.1.call-done = bf16[2048,2048]{1,0:T(8,128)(2,1)} async-done(((bf16[64,2048]{1,0:T(8,128)(2,1)}), bf16[2048,2048]{1,0:T(8,128)(2,1)}) %all-gather.20.cloned.1.call-update) | async-done | bytes 8388624 | tf_op jit(solution)/shard_map/all_gather | solution.py:166
  216.2 15.4 reduce.1
  245.0 63.4 %all-gather.22.cloned.1.call-done = bf16[2048,2048]{1,0:T(8,128)(2,1)} async-done(((bf16[64,2048]{1,0:T(8,128)(2,1)}), bf16[2048,2048]{1,0:T(8,128)(2,1)}) %all-gather.22.cloned.1.call-update) | async-done | bytes 8388624 | tf_op jit(solution)/shard_map/all_gather | solution.py:167
  329.0 15.4 reduce.2
  385.0 41.9 %all-to-all-done.2 = bf16[4,2,131072]{2,1,0:T(2,128)(2,1)} async-done(((bf16[4,2,131072]{2,1,0:T(2,128)(2,1)}), bf16[4,2,131072]{2,1,0:T(2,128)(2,1)}, u32[]{:S(2)}, u32[]{:S(2)}) %all-to-all-start.2) | async-done | bytes 2097184 | tf_op jit(solution)/shard_map/all_to_all | solution.py:183
  449.3 74.4 %while.47 = (s32[]{:T(128)}, bf16[4,512,4,128]{3,2,1,0:T(4,128)(2,1)}, f32[4,4,512]{2,1,0:T(4,128)}, s32[4]{0:T(128)S(1)}, s32[2048]{0:T(1024)S(1)}, /*index=5*/...) while((s32[]{:T(128)}, ...), condition=%wide.region_4.5_spmd, body=%wide.region_1.4_spmd.sunk | while | flops 2201221632 | bytes 69291224 | solution.py:74
  536.9 15.4 reduce.3
  560.5 67.3 %all-to-all-done.3 = bf16[4,2,131072]{2,1,0:T(2,128)(2,1)S(1)} async-done(((bf16[4,2,131072]{2,1,0:T(2,128)(2,1)}), bf16[4,2,131072]{2,1,0:T(2,128)(2,1)S(1)}, u32[]{:S(2)}, u32[]{:S(2)}) %all-to-all-start.3) | async-done | bytes 2097184 | tf_op jit(solution)/shard_map/all_to_all | solution.py:199
  651.8 23.1 reshape.381
  674.9 19.3 fusion.75
  694.2 46.0 %all-gather.40.cloned.1.call-done = bf16[32,172,2048]{2,1,0:T(8,128)(2,1)} async-done(((bf16[1,172,2048]{2,1,0:T(8,128)(2,1)}), bf16[32,172,2048]{2,1,0:T(8,128)(2,1)}) %all-gather.40.cloned.1.call-update) | async-done | bytes 22544400 | tf_op jit(solution)/shard_map/all_gather | solution.py:211
  740.1 22.2 reshape.383
  762.4 19.0 fusion.76
  781.4 104.4 %all-gather.42.cloned.1.call-done = bf16[32,172,2048]{2,1,0:T(8,128)(2,1)} async-done(((bf16[1,172,2048]{2,1,0:T(8,128)(2,1)}), bf16[32,172,2048]{2,1,0:T(8,128)(2,1)}) %all-gather.42.cloned.1.call-update) | async-done | bytes 22544400 | tf_op jit(solution)/shard_map/all_gather | solution.py:222
  885.8 22.4 reshape.385
  908.2 26.8 multiply_convert_fusion.1
  935.1 19.6 fusion.77
  954.7 21.9 multiply_reduce_fusion.1
  998.3 15.4 reduce.4
  1030.2 83.2 %all-to-all-done.4 = bf16[4,2,131072]{2,1,0:T(2,128)(2,1)} async-done(((bf16[4,2,131072]{2,1,0:T(2,128)(2,1)}), bf16[4,2,131072]{2,1,0:T(2,128)(2,1)}, u32[]{:S(2)}, u32[]{:S(2)}) %all-to-all-start.4) | async-done | bytes 2097184 | tf_op jit(solution)/shard_map/all_to_all | solution.py:248
  1134.0 273.0 %while.48 = (s32[]{:T(128)}, f32[2048,4,128]{0,2,1:T(8,128)}, f32[2048,4,128]{0,2,1:T(8,128)}, bf16[4,512,4,128]{3,2,1,0:T(4,128)(2,1)}, s32[4]{0:T(128)S(1)}, /...) while((s32[]{:T(128)}, f32[2048,4,128]{0,2,1:T(8,128)}, ...), condition=%wide.region_9.10_spmd.clone, body=%wide.region_7.9_spmd.clone.sunk | while | flops 5440535040 | bytes 193538896 | solution.py:115
  1163.3 15.0 multiply_convert_fusion.9
  1229.6 15.1 multiply_convert_fusion.9
  1298.4 15.2 multiply_convert_fusion.9
  1367.3 14.8 multiply_convert_fusion.9
  1445.1 40.7 %all-to-all-done.6 = bf16[4,2,131072]{2,1,0:T(2,128)(2,1)S(1)} async-done(((bf16[4,2,131072]{2,1,0:T(2,128)(2,1)}), bf16[4,2,131072]{2,1,0:T(2,128)(2,1)S(1)}, u32[]{:S(2)}, u32[]{:S(2)}) %all-to-all-start.6) | async-done | bytes 2097184 | tf_op jit(solution)/shard_map/all_to_all | solution.py:268
  1502.1 69.5 %all-to-all-done.9 = bf16[512,8,4,64]{0,3,1,2:T(8,128)(2,1)} async-done(((bf16[512,8,4,64]{0,3,1,2:T(8,128)(2,1)}), bf16[512,8,4,64]{0,3,1,2:T(8,128)(2,1)}, u32[]{:S(2)}, u32[]{:S(2)}) %all-to-all-start.9) | async-done | bytes 2097184 | tf_op jit(solution)/shard_map/all_to_all | solution.py:298
  1599.0 74.9 %all-to-all-done.10 = bf16[512,8,4,64]{0,3,1,2:T(8,128)(2,1)} async-done(((bf16[512,8,4,64]{0,3,1,2:T(8,128)(2,1)}), bf16[512,8,4,64]{0,3,1,2:T(8,128)(2,1)}, u32[]{:S(2)}, u32[]{:S(2)}) %all-to-all-start.10) | async-done | bytes 2097184 | tf_op jit(solution)/shard_map/all_to_all | solution.py:299
  1688.4 14.1 reduce.7
  1705.2 50.2 %all-to-all-done.5 = bf16[4,2,131072]{2,1,0:T(2,128)(2,1)} async-done(((bf16[4,2,131072]{2,1,0:T(2,128)(2,1)}), bf16[4,2,131072]{2,1,0:T(2,128)(2,1)}, u32[]{:S(2)}, u32[]{:S(2)}) %all-to-all-start.5) | async-done | bytes 2097184 | tf_op jit(solution)/shard_map/all_to_all | solution.py:267
  1759.2 29.0 reshape.390
  1788.2 14.5 copy.186
  1864.5 29.1 reshape.391
  1893.6 14.5 copy.189
  1908.1 168.1 %all-to-all-done.11 = bf16[512,8,4,172]{0,1,3,2:T(8,128)(2,1)} async-done(((bf16[512,8,4,172]{0,1,3,2:T(8,128)(2,1)}), bf16[512,8,4,172]{0,1,3,2:T(8,128)(2,1)}, u32[]{:S(2)}, u32[]{:S(2)}) %all-to-all-start.11) | async-done | bytes 5636128 | tf_op jit(solution)/shard_map/all_to_all | solution.py:301
  2081.4 19.8 fusion.57
  2102.0 91.9 %collective-permute-done.1 = bf16[512,8,1,172]{0,1,3,2:T(8,128)(2,1)} collective-permute-done((bf16[512,8,1,172]{0,1,3,2:T(8,128)(2,1)}, bf16[512,8,1,172]{0,1,3,2:T(8,128)(2,1)}, u32[]{:S(2)}, u32[]{:S(2)}) %collective-permute-start.1) | collective-permute-done | bytes 1409056 | tf_op jit(solution)/shard_map/ppermute | solution.py:28
  2223.5 18.0 fusion.41
  2273.8 73.7 %all-reduce.4 = (bf16[2048]{0:T(1024)(128)(2,1)S(1)}, bf16[2048]{0:T(1024)(128)(2,1)S(1)}) all-reduce(f32[2048]{0:T(1024)S(1)} %get-tuple-element.284, f32[2048]{0:T(1024)S(1)} %copy-done.32), channel_id=1, replica_groups=mesh['dp'=8,'seq'=4] {'seq'}, use_global_device_ids=true, to_apply=%region_12.13 | all-reduce | flops 4096 | bytes 24576 | tf_op jit(solution)/shard_map/psum | solution.py:291
  2395.4 18.1 fusion.44
  2413.4 18.1 fusion.47
  2475.1 147.6 %concatenate.4 = bf16[8,774,2048]{2,1,0:T(8,128)(2,1)} concatenate(bf16[8,64,2048]{2,1,0:T(8,128)(2,1)} %fusion.51, bf16[8,64,2048]{2,1,0:T(8,128)(2,1)} %bitcast.358, bf16[8,64,2048]{2,1,0:T(8,128)(2,1)} %bitcast.359, bf16[8,64,2048]{2,1,0:T(8,128)(2,1)} %fusion.54, bf16[8,1,2048]{2,1,0:T(2,128)(2,1)S(1)} %broadcast_in_dim.84, bf16[8,172,2048]{2,1,0:T(8,128)(2,1)} %fusion.41, ...), dimensions={1} | concatenate | bytes 50724864 | tf_op jit(solution)/shard_map/concatenate | solution.py:321
  2622.7 25.0 convert_element_type.114
  2647.7 253.6 %fusion = bf16[784,2048]{1,0:T(8,128)(2,1)} fusion(bf16[6192,2048]{1,0:T(8,128)(2,1)} %convert_element_type.114), kind=kCustom, calls=%all-reduce-scatter | all-reduce-scatter fusion | flops 12845057 | bytes 28574208
  2914.7 16.2 concatenate.5
  (359 shorter events, 870.9 us)
Async XLA Ops:
  7.2 49.1 %copy-start.7 = (bf16[1,512,2048]{2,1,0:T(8,128)(2,1)S(1)}, bf16[1,512,2048]{2,1,0:T(8,128)(2,1)}, u32[]{:S(2)}) copy-start(bf16[1,512,2048]{2,1,0:T(8,128)(2,1)} %param.17) | copy-start | bytes 6291460
  7.2 83.9 %all-gather.18.cloned.1.call-start = ((), (), s32[]{:S(2)}) async-start(), calls=%async_computation.13 | async-start | bytes 8650752 | tf_op jit(solution)/shard_map/all_gather | solution.py:165
  7.9 187.6 %all-gather.20.cloned.1.call-start = ((), (), s32[]{:S(2)}) async-start(), calls=%async_computation.14 | async-start | bytes 8650752 | tf_op jit(solution)/shard_map/all_gather | solution.py:166
  8.7 299.7 %all-gather.22.cloned.1.call-start = ((), (), s32[]{:S(2)}) async-start(), calls=%async_computation.15 | async-start | bytes 8650752 | tf_op jit(solution)/shard_map/all_gather | solution.py:167
  9.4 630.0 %all-gather.24.cloned.1.call-start = ((), (), s32[]{:S(2)}) async-start(), calls=%async_computation.16 | async-start | bytes 8650752 | tf_op jit(solution)/shard_map/all_gather | solution.py:203
  10.0 641.8 %all-gather.38.cloned.1.call-start = ((), (), s32[]{:S(2)}) async-start(), calls=%async_computation.23 | async-start | bytes 23789568 | tf_op jit(solution)/shard_map/all_gather | solution.py:211
  10.6 729.6 %all-gather.40.cloned.1.call-start = ((), (), s32[]{:S(2)}) async-start(), calls=%async_computation.24 | async-start | bytes 23789568 | tf_op jit(solution)/shard_map/all_gather | solution.py:211
  11.1 874.6 %all-gather.42.cloned.1.call-start = ((), (), s32[]{:S(2)}) async-start(), calls=%async_computation.25 | async-start | bytes 23789568 | tf_op jit(solution)/shard_map/all_gather | solution.py:222
  56.3 44.1 %copy-start.23 = (f32[2048]{0:T(1024)}, f32[2048]{0:T(1024)S(1)}, u32[]{:S(2)}) copy-start(f32[2048]{0:T(1024)S(1)} %convert_element_type.95) | copy-start | bytes 24580
  56.8 43.6 %copy-start.25 = (f32[512]{0:T(512)}, f32[512]{0:T(512)S(1)}, u32[]{:S(2)}) copy-start(f32[512]{0:T(512)S(1)} %add_rsqrt_fusion.1) | copy-start | bytes 6148
  128.4 107.6 %all-to-all-start = ((bf16[4,2,131072]{2,1,0:T(2,128)(2,1)}), bf16[4,2,131072]{2,1,0:T(2,128)(2,1)S(1)}, u32[]{:S(2)}, u32[]{:S(2)}) async-start(bf16[4,2,131072]{2,1,0:T(2,128)(2,1)} %reshape.393), calls=%async_computation | async-start | bytes 4194304 | tf_op jit(solution)/shard_map/all_to_all | solution.py:177
  236.1 112.8 %all-to-all-start.1 = ((bf16[4,2,131072]{2,1,0:T(2,128)(2,1)}), bf16[4,2,131072]{2,1,0:T(2,128)(2,1)}, u32[]{:S(2)}, u32[]{:S(2)}) async-start(bf16[4,2,131072]{2,1,0:T(2,128)(2,1)} %reshape.395), calls=%async_computation.1 | async-start | bytes 4194304 | tf_op jit(solution)/shard_map/all_to_all | solution.py:180
  348.9 78.0 %all-to-all-start.2 = ((bf16[4,2,131072]{2,1,0:T(2,128)(2,1)}), bf16[4,2,131072]{2,1,0:T(2,128)(2,1)}, u32[]{:S(2)}, u32[]{:S(2)}) async-start(bf16[4,2,131072]{2,1,0:T(2,128)(2,1)} %reshape.397), calls=%async_computation.2 | async-start | bytes 4194304 | tf_op jit(solution)/shard_map/all_to_all | solution.py:183
  523.7 28.5 copy-start.1
  556.8 71.0 %all-to-all-start.3 = ((bf16[4,2,131072]{2,1,0:T(2,128)(2,1)}), bf16[4,2,131072]{2,1,0:T(2,128)(2,1)S(1)}, u32[]{:S(2)}, u32[]{:S(2)}) async-start(bf16[4,2,131072]{2,1,0:T(2,128)(2,1)} %reshape.399), calls=%async_computation.3 | async-start | bytes 4194304 | tf_op jit(solution)/shard_map/all_to_all | solution.py:199
  560.4 1663.1 %all-gather.34.cloned.1.call-start = ((), (), s32[]{:S(2)}) async-start(), calls=%async_computation.21 | async-start | bytes 10485760 | tf_op jit(solution)/shard_map/all_gather | solution.py:313
  560.4 86.8 %copy-start.17 = (f32[2048]{0:T(1024)}, f32[2048]{0:T(1024)S(1)}, u32[]{:S(2)}) copy-start(f32[2048]{0:T(1024)S(1)} %convert_element_type.100) | copy-start | bytes 24580
  651.0 1762.4 %all-gather.36.cloned.1.call-start = ((), (), s32[]{:S(2)}) async-start(), calls=%async_computation.22 | async-start | bytes 10485760 | tf_op jit(solution)/shard_map/all_gather | solution.py:314
  651.7 23.1 copy-start.12
  781.4 126.8 %copy-start.11 = (bf16[1,512,2048]{2,1,0:T(8,128)(2,1)S(1)}, bf16[1,512,2048]{2,1,0:T(8,128)(2,1)}, u32[]{:S(2)}) copy-start(bf16[1,512,2048]{2,1,0:T(8,128)(2,1)} %param.29) | copy-start | bytes 6291460
  935.1 19.7 copy-start.6
  935.1 19.7 copy-start.18
  935.1 19.7 copy-start.21
  1013.7 9.2 copy-start.31
  1013.7 9.3 copy-start.9
  1018.4 95.0 %all-to-all-start.4 = ((bf16[4,2,131072]{2,1,0:T(2,128)(2,1)}), bf16[4,2,131072]{2,1,0:T(2,128)(2,1)}, u32[]{:S(2)}, u32[]{:S(2)}) async-start(bf16[4,2,131072]{2,1,0:T(2,128)(2,1)} %reshape.401), calls=%async_computation.4 | async-start | bytes 4194304 | tf_op jit(solution)/shard_map/all_to_all | solution.py:248
  1022.8 1408.7 %all-gather.32.cloned.1.call-start = ((), (), s32[]{:S(2)}) async-start(), calls=%async_computation.20 | async-start | bytes 10485760 | tf_op jit(solution)/shard_map/all_gather | solution.py:312
  1113.4 320.6 %all-to-all-start.8 = ((bf16[512,8,4,64]{0,3,1,2:T(8,128)(2,1)}), bf16[512,8,4,64]{0,3,1,2:T(8,128)(2,1)}, u32[]{:S(2)}, u32[]{:S(2)}) async-start(bf16[512,8,4,64]{0,3,1,2:T(8,128)(2,1)} %copy.170), calls=%async_computation.8 | async-start | bytes 4194304 | tf_op jit(solution)/shard_map/all_to_all | solution.py:297
  1433.9 51.8 %all-to-all-start.6 = ((bf16[4,2,131072]{2,1,0:T(2,128)(2,1)}), bf16[4,2,131072]{2,1,0:T(2,128)(2,1)S(1)}, u32[]{:S(2)}, u32[]{:S(2)}) async-start(bf16[4,2,131072]{2,1,0:T(2,128)(2,1)} %reshape.405), calls=%async_computation.6 | async-start | bytes 4194304 | tf_op jit(solution)/shard_map/all_to_all | solution.py:268
  1485.7 85.8 %all-to-all-start.9 = ((bf16[512,8,4,64]{0,3,1,2:T(8,128)(2,1)}), bf16[512,8,4,64]{0,3,1,2:T(8,128)(2,1)}, u32[]{:S(2)}, u32[]{:S(2)}) async-start(bf16[512,8,4,64]{0,3,1,2:T(8,128)(2,1)} %copy.173), calls=%async_computation.9 | async-start | bytes 4194304 | tf_op jit(solution)/shard_map/all_to_all | solution.py:298
  1490.2 951.4 %all-gather.28.cloned.1.call-start = ((), (), s32[]{:S(2)}) async-start(), calls=%async_computation.18 | async-start | bytes 10485760 | tf_op jit(solution)/shard_map/all_gather | solution.py:310
  1498.7 77.3 %copy-start.13 = (bf16[4,512,4,128]{3,2,1,0:T(4,128)(2,1)S(1)}, bf16[4,512,4,128]{3,2,1,0:T(4,128)(2,1)}, u32[]{:S(2)}) copy-start(bf16[4,512,4,128]{3,2,1,0:T(4,128)(2,1)} %get-tuple-element.167) | copy-start | bytes 6291460
  1571.6 102.3 %all-to-all-start.10 = ((bf16[512,8,4,64]{0,3,1,2:T(8,128)(2,1)}), bf16[512,8,4,64]{0,3,1,2:T(8,128)(2,1)}, u32[]{:S(2)}, u32[]{:S(2)}) async-start(bf16[512,8,4,64]{0,3,1,2:T(8,128)(2,1)} %copy.176), calls=%async_computation.10 | async-start | bytes 4194304 | tf_op jit(solution)/shard_map/all_to_all | solution.py:299
  1673.9 81.5 %all-to-all-start.5 = ((bf16[4,2,131072]{2,1,0:T(2,128)(2,1)}), bf16[4,2,131072]{2,1,0:T(2,128)(2,1)}, u32[]{:S(2)}, u32[]{:S(2)}) async-start(bf16[4,2,131072]{2,1,0:T(2,128)(2,1)} %reshape.403), calls=%async_computation.5 | async-start | bytes 4194304 | tf_op jit(solution)/shard_map/all_to_all | solution.py:267
  1755.4 50.7 %all-to-all-start.7 = ((bf16[4,2,131072]{2,1,0:T(2,128)(2,1)}), bf16[4,2,131072]{2,1,0:T(2,128)(2,1)S(1)}, u32[]{:S(2)}, u32[]{:S(2)}) async-start(bf16[4,2,131072]{2,1,0:T(2,128)(2,1)} %reshape.407), calls=%async_computation.7 | async-start | bytes 4194304 | tf_op jit(solution)/shard_map/all_to_all | solution.py:269
  1806.1 270.1 %all-to-all-start.11 = ((bf16[512,8,4,172]{0,1,3,2:T(8,128)(2,1)}), bf16[512,8,4,172]{0,1,3,2:T(8,128)(2,1)}, u32[]{:S(2)}, u32[]{:S(2)}) async-start(bf16[512,8,4,172]{0,1,3,2:T(8,128)(2,1)} %copy.186), calls=%async_computation.11 | async-start | bytes 11272192 | tf_op jit(solution)/shard_map/all_to_all | solution.py:301
  1811.3 640.1 %all-gather.30.cloned.1.call-start = ((), (), s32[]{:S(2)}) async-start(), calls=%async_computation.19 | async-start | bytes 10485760 | tf_op jit(solution)/shard_map/all_gather | solution.py:311
  1857.2 244.8 %collective-permute-start = (bf16[512,8,1,172]{0,1,3,2:T(8,128)(2,1)S(1)}, bf16[512,8,1,172]{0,1,3,2:T(8,128)(2,1)}, u32[]{:S(2)}, u32[]{:S(2)}) collective-permute-start(bf16[512,8,1,172]{0,1,3,2:T(8,128)(2,1)S(1)} %bitcast.364), channel_id=1, source_target_pairs={{0,1},{1,0},{2,3},{3,2},{4,5},{5,4},{6,7},{7,6},{8,9},{9,8},{10,11... | collective-permute-start | bytes 4227080 | tf_op jit(solution)/shard_map/ppermute | solution.py:28
  1860.4 333.5 %collective-permute-start.1 = (bf16[512,8,1,172]{0,1,3,2:T(8,128)(2,1)}, bf16[512,8,1,172]{0,1,3,2:T(8,128)(2,1)}, u32[]{:S(2)}, u32[]{:S(2)}) collective-permute-start(bf16[512,8,1,172]{0,1,3,2:T(8,128)(2,1)} %bitcast.280), channel_id=1, source_target_pairs={{0,2},{1,3},{2,0},{3,1},{4,6},{5,7},{6,4},{7,5},{8,10},{9,11},{10,... | collective-permute-start | bytes 4227080 | tf_op jit(solution)/shard_map/ppermute | solution.py:28
  1864.3 329.6 %collective-permute-start.2 = (bf16[512,8,1,172]{0,1,3,2:T(8,128)(2,1)}, bf16[512,8,1,172]{0,1,3,2:T(8,128)(2,1)}, u32[]{:S(2)}, u32[]{:S(2)}) collective-permute-start(bf16[512,8,1,172]{0,1,3,2:T(8,128)(2,1)} %bitcast.279), channel_id=1, source_target_pairs={{0,3},{1,2},{2,1},{3,0},{4,7},{5,6},{6,5},{7,4},{8,11},{9,10},{10,... | collective-permute-start | bytes 4227080 | tf_op jit(solution)/shard_map/ppermute | solution.py:28
  2076.2 301.3 %all-to-all-start.12 = ((bf16[512,8,4,172]{0,1,3,2:T(8,128)(2,1)}), bf16[512,8,4,172]{0,1,3,2:T(8,128)(2,1)}, u32[]{:S(2)}, u32[]{:S(2)}) async-start(bf16[512,8,4,172]{0,1,3,2:T(8,128)(2,1)} %copy.189), calls=%async_computation.12 | async-start | bytes 11272192 | tf_op jit(solution)/shard_map/all_to_all | solution.py:302
  2081.4 383.6 %all-gather.26.cloned.1.call-start = ((), (), s32[]{:S(2)}) async-start(), calls=%async_computation.17 | async-start | bytes 10485760 | tf_op jit(solution)/shard_map/all_gather | solution.py:309
  2253.1 11.0 copy-start.14
  2264.2 9.6 copy-start.32
  2647.7 259.0 %copy-start.19 = (f32[2048]{0:T(1024)S(1)}, f32[2048]{0:T(1024)}, u32[]{:S(2)}) copy-start(f32[2048]{0:T(1024)} %copy-done.17) | copy-start | bytes 24580
  2647.7 259.0 %copy-start.22 = (f32[512]{0:T(512)S(1)}, f32[512]{0:T(512)}, u32[]{:S(2)}) copy-start(f32[512]{0:T(512)} %copy-done.20) | copy-start | bytes 6148
  2647.7 259.0 %copy-start.29 = (f32[512]{0:T(512)S(1)}, f32[512]{0:T(512)}, u32[]{:S(2)}) copy-start(f32[512]{0:T(512)} %copy-done.28) | copy-start | bytes 6148
  2902.3 12.4 collective-permute-start.3
  (26 other events, 118.5 us)
Sparse Core Ops, SparseCore 0:
  11.0 80.1 all-gather.17
  94.0 101.4 all-gather.19
  198.5 109.8 all-gather.21
  311.2 108.5 all-gather.23
  422.5 161.4 all-gather.37
  586.7 153.4 all-gather.39
  743.0 142.7 all-gather.41
  887.4 164.3 all-gather.33
  1053.4 206.5 all-gather.35
  1261.4 147.7 all-gather.31
  1498.9 271.1 all-gather.27
  1820.0 349.5 all-gather.29
  2253.2 211.6 all-gather.25
